TPU v7x, 32 devices: a whole 2x2x4 slice. The times are simulated.
32 devices in a mesh: ka: 16 (over z, x, core), ga: 2 (over y).
Axes of the slice: x: 2, y: 2, z: 4, core: 2. Of those that a mesh axis runs over, the one named last changes fastest.
Arguments:
- pair_density: bfloat16 [256, 64, 4096], P('ka', None, 'ga'), may hold values from -0.1875 to 0.1875
- trial_vectors: bfloat16 [256, 64, 128], P('ka'), may hold values from -6 to 6
- energy: float32 [256, 64], P('ka'), may hold values from 0.5 to 2.5
- coulomb: float32 [4096], P('ga'), may hold values from 0.03 to 0.3
- screen: bfloat16 [32, 4096, 256], P(None, 'ga'), may hold values from -0.375 to 0.375
- neighbors: int32 [256, 16], P('ka'), may hold values from 0 to 255, as said below
- live_count: int32 [256], P('ka'), may hold values from 1 to 16, as said below
- q_index: int32 [256, 16], P('ka'), may hold values from 0 to 31
Outputs:
- applied: bfloat16 [256, 64, 128], P('ka', 'ga')
Inputs may be any that keep to these rules, and one draw needn't show every extreme that they name: `neighbors`: the 16 partners of k-point k are distinct k-points whose block k' // 16 is the block of k or one of its two neighbours on the closed cycle of 16 blocks. Only the first live_count[k] slots of row k of neighbors and q_index are used; some k-point uses all 16.
All inputs are finite; a program needn't handle non-finite values.
Results may differ from a plain program's by a relative error of at most 0.013.
Values may be sent and summed in bfloat16 or wider, within the bound.
No kernel may reach another device: no remote copies, remote signals or barrier semaphores. Data moves between devices by JAX's collectives and lax.ppermute only.
A program may use at most 192 MiB of HBM per device.

v0:
```python
import jax
import jax.numpy as jnp
from jax import lax
from jax.sharding import PartitionSpec as P


def passed_along(value, axis, steps):
    count = lax.axis_size(axis)
    pairs = [(source, (source + steps) % count) for source in range(count)]
    return lax.ppermute(value, axis, pairs)


def form_products(density, vectors):
    return jnp.einsum("kpg,kpt->kgt", density, vectors, preferred_element_type=jnp.float32).astype(
        jnp.bfloat16
    )


def on_device(pair_density, trial_vectors, energy, coulomb, screen, neighbors, live_count, q_index):
    local_k, pair_count, local_g = pair_density.shape
    trial_count = trial_vectors.shape[2]
    block_size = screen.shape[2]
    groups = local_g // block_size
    cycle_size = lax.axis_size("ka")
    position = lax.axis_index("ka")
    own_products = form_products(pair_density, trial_vectors)
    below_block = passed_along(own_products, "ka", 1)
    above_block = passed_along(own_products, "ka", -1)
    window = jnp.concatenate([below_block, own_products, above_block], axis=0)
    partial_value = jnp.sum(own_products, axis=0, dtype=jnp.float32)
    density_total = lax.psum(partial_value, "ka")
    screened = coulomb[:, None] * density_total
    offset = (neighbors // local_k - position + 1) % cycle_size
    local_index = offset * local_k + neighbors % local_k

    def add_slot(slot_index, summed):
        picked = jnp.take(window, local_index[:, slot_index], axis=0)
        blocks = jnp.take(screen, q_index[:, slot_index], axis=0)
        coupled = jnp.einsum(
            "kbgc,kbct->kbgt",
            blocks.reshape(local_k, groups, block_size, block_size),
            picked.reshape(local_k, groups, block_size, trial_count),
            preferred_element_type=jnp.float32,
        ).reshape(local_k, local_g, trial_count)
        is_live = (slot_index < live_count)[:, None, None]
        return summed + jnp.where(is_live, coupled, 0.0)

    last_slot = neighbors.shape[1]
    direct = lax.fori_loop(
        0, last_slot, add_slot, jnp.zeros((local_k, local_g, trial_count), jnp.float32)
    )
    kernel = (2.0 * screened[None] - direct).astype(jnp.bfloat16)
    pair_terms = jnp.einsum(
        "kpg,kgt->kpt", pair_density, kernel, preferred_element_type=jnp.float32
    )
    mine = lax.psum_scatter(pair_terms, "ga", scatter_dimension=1, tiled=True)
    row_count = mine.shape[1]
    first_row = lax.axis_index("ga") * row_count
    energy_rows = lax.dynamic_slice_in_dim(energy, first_row, row_count, 1)
    vector_rows = lax.dynamic_slice_in_dim(trial_vectors, first_row, row_count, 1)
    return (energy_rows[:, :, None] * vector_rows.astype(jnp.float32) + mine).astype(jnp.bfloat16)


def solution(mesh):
    in_specs = (
        P("ka", None, "ga"),
        P("ka", None, None),
        P("ka", None),
        P("ga"),
        P(None, "ga", None),
        P("ka", None),
        P("ka"),
        P("ka", None),
    )
    out_specs = P("ka", "ga", None)
    return jax.shard_map(
        on_device, mesh=mesh, in_specs=in_specs, out_specs=out_specs, check_vma=False
    )
```

profile of v0, /device:TPU:0, one launch (start us, length us, event | category | flops | bytes accessed | tf_op | source)
XLA Modules:
  0.0 1172.0 jit_solution(3300030302084759185)
XLA Ops:
  23.2 165.4 %all-reduce.2.cloned.1.call-done = f32[2048,128]{1,0:T(8,128)} async-done(((f32[2048,128]{1,0:T(8,128)}), f32[2048,128]{1,0:T(8,128)}) %all-reduce.2.cloned.1.call-update) | async-done | bytes 1048592 | tf_op jit(solution)/shard_map/psum | solution.py:31
  191.1 17.6 %pad_maximum_fusion = bf16[48,2048,128]{2,1,0:T(8,128)(2,1)} fusion(bf16[16,2048,128]{2,1,0:T(8,128)(2,1)} %collective-permute-done.1, bf16[16,2048,128]{2,1,0:T(8,128)(2,1)} %get-tuple-element.182, bf16[16,2048,128]{2,1,0:T(8,128)(2,1)} %collective-permute-done), kind=kLoop, calls=%fused_computation.19 | loop fusion | flops 25165824 | bytes 50331648 | tf_op jit(solution)/shard_map/concatenate | solution.py:29
  208.7 909.0 %while.14 = (s32[]{:T(128)}, f32[16,2048,128]{2,1,0:T(8,128)}, s32[16]{0:T(128)S(1)}, s32[16,16]{0,1:T(8,128)S(1)}, bf16[32,2048,256]{2,1,0:T(8,128)(2,1)}, /*in...) while((s32[]{:T(128)}, f32[16,2048,128]{2,1,0:T(8,128)}, ...), condition=%wide.region_3.4_spmd.clone, body=%wide.region_2.3_spmd.clone.sunk | while | flops 2172651776 | bytes 142615312 | solution.py:49
  299.3 17.8 %fusion.28 = f32[16,2048,128]{2,1,0:T(8,128)} fusion(f32[16,8,256,128]{3,2,1,0:T(8,128)} %fusion.27, f32[16,2048,128]{2,1,0:T(8,128)} %get-tuple-element.244, pred[16]{0:T(512)(128)(4,1)S(1)} %broadcast_compare_fusion.2, pred[]{:T(512)S(6)} %compare.7), kind=kLoop, calls=%fused_computation.3.clone.1 | loop fusion | flops 12582912 | bytes 50331664 | tf_op jit(solution)/shard_map/while/body/eval_jaxpr/add | solution.py:46
  356.0 17.8 %fusion.28 = f32[16,2048,128]{2,1,0:T(8,128)} fusion(f32[16,8,256,128]{3,2,1,0:T(8,128)} %fusion.27, f32[16,2048,128]{2,1,0:T(8,128)} %get-tuple-element.244, pred[16]{0:T(512)(128)(4,1)S(1)} %broadcast_compare_fusion.2, pred[]{:T(512)S(6)} %compare.7), kind=kLoop, calls=%fused_computation.3.clone.1 | loop fusion | flops 12582912 | bytes 50331664 | tf_op jit(solution)/shard_map/while/body/eval_jaxpr/add | solution.py:46
  413.0 17.8 %fusion.28 = f32[16,2048,128]{2,1,0:T(8,128)} fusion(f32[16,8,256,128]{3,2,1,0:T(8,128)} %fusion.27, f32[16,2048,128]{2,1,0:T(8,128)} %get-tuple-element.244, pred[16]{0:T(512)(128)(4,1)S(1)} %broadcast_compare_fusion.2, pred[]{:T(512)S(6)} %compare.7), kind=kLoop, calls=%fused_computation.3.clone.1 | loop fusion | flops 12582912 | bytes 50331664 | tf_op jit(solution)/shard_map/while/body/eval_jaxpr/add | solution.py:46
  455.6 14.0 %fusion.27 = f32[16,8,256,128]{3,2,1,0:T(8,128)} fusion(bf16[16,8,256,256]{3,2,1,0:T(8,128)(2,1)} %bitcast.29, pred[16]{0:T(512)(128)(4,1)S(1)} %get-tuple-element.231, bf16[16,8,256,128]{3,2,1,0:T(8,128)(2,1)} %bitcast.30, pred[16]{0:T(512)(128)(4,1)S(1)} %get-tuple-element.233), kind=kOutput, calls=%fused_computation.4.clone.1 | convolution fusion | flops 2160066560 | bytes 41943072 | tf_op jit(solution)/shard_map/while/body/eval_jaxpr/kbgc,kbct->kbgt/dot_general | solution.py:39
  469.6 17.8 %fusion.28 = f32[16,2048,128]{2,1,0:T(8,128)} fusion(f32[16,8,256,128]{3,2,1,0:T(8,128)} %fusion.27, f32[16,2048,128]{2,1,0:T(8,128)} %get-tuple-element.244, pred[16]{0:T(512)(128)(4,1)S(1)} %broadcast_compare_fusion.2, pred[]{:T(512)S(6)} %compare.7), kind=kLoop, calls=%fused_computation.3.clone.1 | loop fusion | flops 12582912 | bytes 50331664 | tf_op jit(solution)/shard_map/while/body/eval_jaxpr/add | solution.py:46
  512.3 14.0 %fusion.27 = f32[16,8,256,128]{3,2,1,0:T(8,128)} fusion(bf16[16,8,256,256]{3,2,1,0:T(8,128)(2,1)} %bitcast.29, pred[16]{0:T(512)(128)(4,1)S(1)} %get-tuple-element.231, bf16[16,8,256,128]{3,2,1,0:T(8,128)(2,1)} %bitcast.30, pred[16]{0:T(512)(128)(4,1)S(1)} %get-tuple-element.233), kind=kOutput, calls=%fused_computation.4.clone.1 | convolution fusion | flops 2160066560 | bytes 41943072 | tf_op jit(solution)/shard_map/while/body/eval_jaxpr/kbgc,kbct->kbgt/dot_general | solution.py:39
  526.3 17.8 %fusion.28 = f32[16,2048,128]{2,1,0:T(8,128)} fusion(f32[16,8,256,128]{3,2,1,0:T(8,128)} %fusion.27, f32[16,2048,128]{2,1,0:T(8,128)} %get-tuple-element.244, pred[16]{0:T(512)(128)(4,1)S(1)} %broadcast_compare_fusion.2, pred[]{:T(512)S(6)} %compare.7), kind=kLoop, calls=%fused_computation.3.clone.1 | loop fusion | flops 12582912 | bytes 50331664 | tf_op jit(solution)/shard_map/while/body/eval_jaxpr/add | solution.py:46
  583.1 17.8 %fusion.28 = f32[16,2048,128]{2,1,0:T(8,128)} fusion(f32[16,8,256,128]{3,2,1,0:T(8,128)} %fusion.27, f32[16,2048,128]{2,1,0:T(8,128)} %get-tuple-element.244, pred[16]{0:T(512)(128)(4,1)S(1)} %broadcast_compare_fusion.2, pred[]{:T(512)S(6)} %compare.7), kind=kLoop, calls=%fused_computation.3.clone.1 | loop fusion | flops 12582912 | bytes 50331664 | tf_op jit(solution)/shard_map/while/body/eval_jaxpr/add | solution.py:46
  640.4 17.8 %fusion.28 = f32[16,2048,128]{2,1,0:T(8,128)} fusion(f32[16,8,256,128]{3,2,1,0:T(8,128)} %fusion.27, f32[16,2048,128]{2,1,0:T(8,128)} %get-tuple-element.244, pred[16]{0:T(512)(128)(4,1)S(1)} %broadcast_compare_fusion.2, pred[]{:T(512)S(6)} %compare.7), kind=kLoop, calls=%fused_computation.3.clone.1 | loop fusion | flops 12582912 | bytes 50331664 | tf_op jit(solution)/shard_map/while/body/eval_jaxpr/add | solution.py:46
  697.0 17.8 %fusion.28 = f32[16,2048,128]{2,1,0:T(8,128)} fusion(f32[16,8,256,128]{3,2,1,0:T(8,128)} %fusion.27, f32[16,2048,128]{2,1,0:T(8,128)} %get-tuple-element.244, pred[16]{0:T(512)(128)(4,1)S(1)} %broadcast_compare_fusion.2, pred[]{:T(512)S(6)} %compare.7), kind=kLoop, calls=%fused_computation.3.clone.1 | loop fusion | flops 12582912 | bytes 50331664 | tf_op jit(solution)/shard_map/while/body/eval_jaxpr/add | solution.py:46
  739.7 14.0 %fusion.27 = f32[16,8,256,128]{3,2,1,0:T(8,128)} fusion(bf16[16,8,256,256]{3,2,1,0:T(8,128)(2,1)} %bitcast.29, pred[16]{0:T(512)(128)(4,1)S(1)} %get-tuple-element.231, bf16[16,8,256,128]{3,2,1,0:T(8,128)(2,1)} %bitcast.30, pred[16]{0:T(512)(128)(4,1)S(1)} %get-tuple-element.233), kind=kOutput, calls=%fused_computation.4.clone.1 | convolution fusion | flops 2160066560 | bytes 41943072 | tf_op jit(solution)/shard_map/while/body/eval_jaxpr/kbgc,kbct->kbgt/dot_general | solution.py:39
  753.7 17.8 %fusion.28 = f32[16,2048,128]{2,1,0:T(8,128)} fusion(f32[16,8,256,128]{3,2,1,0:T(8,128)} %fusion.27, f32[16,2048,128]{2,1,0:T(8,128)} %get-tuple-element.244, pred[16]{0:T(512)(128)(4,1)S(1)} %broadcast_compare_fusion.2, pred[]{:T(512)S(6)} %compare.7), kind=kLoop, calls=%fused_computation.3.clone.1 | loop fusion | flops 12582912 | bytes 50331664 | tf_op jit(solution)/shard_map/while/body/eval_jaxpr/add | solution.py:46
  796.4 14.0 %fusion.27 = f32[16,8,256,128]{3,2,1,0:T(8,128)} fusion(bf16[16,8,256,256]{3,2,1,0:T(8,128)(2,1)} %bitcast.29, pred[16]{0:T(512)(128)(4,1)S(1)} %get-tuple-element.231, bf16[16,8,256,128]{3,2,1,0:T(8,128)(2,1)} %bitcast.30, pred[16]{0:T(512)(128)(4,1)S(1)} %get-tuple-element.233), kind=kOutput, calls=%fused_computation.4.clone.1 | convolution fusion | flops 2160066560 | bytes 41943072 | tf_op jit(solution)/shard_map/while/body/eval_jaxpr/kbgc,kbct->kbgt/dot_general | solution.py:39
  810.4 17.8 %fusion.28 = f32[16,2048,128]{2,1,0:T(8,128)} fusion(f32[16,8,256,128]{3,2,1,0:T(8,128)} %fusion.27, f32[16,2048,128]{2,1,0:T(8,128)} %get-tuple-element.244, pred[16]{0:T(512)(128)(4,1)S(1)} %broadcast_compare_fusion.2, pred[]{:T(512)S(6)} %compare.7), kind=kLoop, calls=%fused_computation.3.clone.1 | loop fusion | flops 12582912 | bytes 50331664 | tf_op jit(solution)/shard_map/while/body/eval_jaxpr/add | solution.py:46
  868.9 17.8 %fusion.28 = f32[16,2048,128]{2,1,0:T(8,128)} fusion(f32[16,8,256,128]{3,2,1,0:T(8,128)} %fusion.27, f32[16,2048,128]{2,1,0:T(8,128)} %get-tuple-element.244, pred[16]{0:T(512)(128)(4,1)S(1)} %broadcast_compare_fusion.2, pred[]{:T(512)S(6)} %compare.7), kind=kLoop, calls=%fused_computation.3.clone.1 | loop fusion | flops 12582912 | bytes 50331664 | tf_op jit(solution)/shard_map/while/body/eval_jaxpr/add | solution.py:46
  927.3 17.8 %fusion.28 = f32[16,2048,128]{2,1,0:T(8,128)} fusion(f32[16,8,256,128]{3,2,1,0:T(8,128)} %fusion.27, f32[16,2048,128]{2,1,0:T(8,128)} %get-tuple-element.244, pred[16]{0:T(512)(128)(4,1)S(1)} %broadcast_compare_fusion.2, pred[]{:T(512)S(6)} %compare.7), kind=kLoop, calls=%fused_computation.3.clone.1 | loop fusion | flops 12582912 | bytes 50331664 | tf_op jit(solution)/shard_map/while/body/eval_jaxpr/add | solution.py:46
  984.4 17.8 %fusion.28 = f32[16,2048,128]{2,1,0:T(8,128)} fusion(f32[16,8,256,128]{3,2,1,0:T(8,128)} %fusion.27, f32[16,2048,128]{2,1,0:T(8,128)} %get-tuple-element.244, pred[16]{0:T(512)(128)(4,1)S(1)} %broadcast_compare_fusion.2, pred[]{:T(512)S(6)} %compare.7), kind=kLoop, calls=%fused_computation.3.clone.1 | loop fusion | flops 12582912 | bytes 50331664 | tf_op jit(solution)/shard_map/while/body/eval_jaxpr/add | solution.py:46
  1042.2 17.8 %fusion.28 = f32[16,2048,128]{2,1,0:T(8,128)} fusion(f32[16,8,256,128]{3,2,1,0:T(8,128)} %fusion.27, f32[16,2048,128]{2,1,0:T(8,128)} %get-tuple-element.244, pred[16]{0:T(512)(128)(4,1)S(1)} %broadcast_compare_fusion.2, pred[]{:T(512)S(6)} %compare.7), kind=kLoop, calls=%fused_computation.3.clone.1 | loop fusion | flops 12582912 | bytes 50331664 | tf_op jit(solution)/shard_map/while/body/eval_jaxpr/add | solution.py:46
  1085.8 14.0 %fusion.27 = f32[16,8,256,128]{3,2,1,0:T(8,128)} fusion(bf16[16,8,256,256]{3,2,1,0:T(8,128)(2,1)} %bitcast.29, pred[16]{0:T(512)(128)(4,1)S(1)} %get-tuple-element.231, bf16[16,8,256,128]{3,2,1,0:T(8,128)(2,1)} %bitcast.30, pred[16]{0:T(512)(128)(4,1)S(1)} %get-tuple-element.233), kind=kOutput, calls=%fused_computation.4.clone.1 | convolution fusion | flops 2160066560 | bytes 41943072 | tf_op jit(solution)/shard_map/while/body/eval_jaxpr/kbgc,kbct->kbgt/dot_general | solution.py:39
  1099.9 17.8 %fusion.28 = f32[16,2048,128]{2,1,0:T(8,128)} fusion(f32[16,8,256,128]{3,2,1,0:T(8,128)} %fusion.27, f32[16,2048,128]{2,1,0:T(8,128)} %get-tuple-element.244, pred[16]{0:T(512)(128)(4,1)S(1)} %broadcast_compare_fusion.2, pred[]{:T(512)S(6)} %compare.7), kind=kLoop, calls=%fused_computation.3.clone.1 | loop fusion | flops 12582912 | bytes 50331664 | tf_op jit(solution)/shard_map/while/body/eval_jaxpr/add | solution.py:46
  1128.9 34.5 %reduce-scatter.2.cloned.1.call-done = f32[16,32,128]{2,1,0:T(8,128)} async-done(((f32[16,64,128]{2,1,0:T(8,128)}), f32[16,32,128]{2,1,0:T(8,128)}) %reduce-scatter.2.cloned.1.call-update) | async-done | bytes 262160 | tf_op jit(solution)/shard_map/reduce_scatter | solution.py:56
  (133 shorter events, 603.1 us)
Async XLA Ops:
  6.5 1122.3 %copy-start = (f32[16,64]{1,0:T(8,128)S(1)}, f32[16,64]{1,0:T(8,128)}, u32[]{:S(2)}) copy-start(f32[16,64]{1,0:T(8,128)} %param.12) | copy-start | bytes 12292
  6.5 182.0 %all-reduce.2.cloned.1.call-start = ((), (), s32[]{:S(2)}) async-start(), calls=%async_computation.1 | async-start | bytes 2097152 | tf_op jit(solution)/shard_map/psum | solution.py:31
  16.1 175.0 %collective-permute-start = (bf16[16,2048,128]{2,1,0:T(8,128)(2,1)}, bf16[16,2048,128]{2,1,0:T(8,128)(2,1)}, u32[]{:S(2)}, u32[]{:S(2)}) collective-permute-start(bf16[16,2048,128]{2,1,0:T(8,128)(2,1)} %get-tuple-element.182), channel_id=1, source_target_pairs={{0,2},{2,4},{4,6},{6,8},{8,10},{10,12},{12,14},{14,16},{16,18},{18... | collective-permute-start | bytes 25165832 | tf_op jit(solution)/shard_map/ppermute | solution.py:10
  16.6 174.5 %collective-permute-start.1 = (bf16[16,2048,128]{2,1,0:T(8,128)(2,1)}, bf16[16,2048,128]{2,1,0:T(8,128)(2,1)}, u32[]{:S(2)}, u32[]{:S(2)}) collective-permute-start(bf16[16,2048,128]{2,1,0:T(8,128)(2,1)} %get-tuple-element.182), channel_id=1, source_target_pairs={{0,30},{2,0},{4,2},{6,4},{8,6},{10,8},{12,10},{14,12},{16,14},{18,... | collective-permute-start | bytes 25165832 | tf_op jit(solution)/shard_map/ppermute | solution.py:10
  21.6 1141.9 %reduce-scatter.2.cloned.1.call-start = ((), (), s32[]{:S(2)}) async-start(), calls=%async_computation.2 | async-start | bytes 786432 | tf_op jit(solution)/shard_map/reduce_scatter | solution.py:56
  191.1 17.6 %copy-start.3 = (s32[16]{0:T(128)S(1)}, s32[16]{0:T(128)}, u32[]{:S(2)}) copy-start(s32[16]{0:T(128)} %param.16) | copy-start | bytes 196
  208.7 909.0 %copy-start.1 = (f32[2048,128]{1,0:T(8,128)S(1)}, f32[2048,128]{1,0:T(8,128)}, u32[]{:S(2)}) copy-start(f32[2048,128]{1,0:T(8,128)} %multiply_multiply_fusion) | copy-start | bytes 3145732
  1117.7 45.7 %copy-start.2 = (bf16[16,64,128]{2,1,0:T(8,128)(2,1)S(1)}, bf16[16,64,128]{2,1,0:T(8,128)(2,1)}, u32[]{:S(2)}) copy-start(bf16[16,64,128]{2,1,0:T(8,128)(2,1)} %param.11) | copy-start | bytes 786436
Sparse Core Ops, SparseCore 0:
  21.7 166.8 all-reduce.1
  1128.9 34.4 reduce-scatter.1
where the time goes:
time: 1170 us
  local copies, waits for them, and re-layouts  406 us (35%)
  other arithmetic  302 us (26%)
  matrix products  245 us (21%)
  waiting for transfers between devices  200 us (17%)
  between operations  13.5 us (1%)
    add x16, other arithmetic, add_slot(): return summed + jnp.where(is_live, coupled, 0.0)  279 us
    dot_general x16, matrix products, add_slot(): jnp.einsum('kbgc,kbct->kbgt', blocks.reshape(local_k, groups, block_size,...  224 us
    gather x16, local copies, waits for them, and re-layouts, add_slot(): picked = jnp.take(window, local_index[:, slot_index], axis=0)  208 us
    gather x16, local copies, waits for them, and re-layouts, add_slot(): blocks = jnp.take(screen, q_index[:, slot_index], axis=0)  197 us
    psum x1, waiting for transfers between devices, on_device(): density_total = lax.psum(partial_value, 'ka')  165 us
    reduce_scatter x1, waiting for transfers between devices, on_device(): mine = lax.psum_scatter(pair_terms, 'ga', scatter_dimension=1, tiled=True)  34.5 us
  transfers between devices with their start and end apart: 4, of which 2 were waited for; matrix products, arithmetic and copies ran while one was open for 0% of the time, Pallas kernels for 0%

commit v1 on v0

--- a/solution.py
+++ b/solution.py
@@ -28,7 +28,11 @@
     above_block = passed_along(own_products, "ka", -1)
     window = jnp.concatenate([below_block, own_products, above_block], axis=0)
     partial_value = jnp.sum(own_products, axis=0, dtype=jnp.float32)
-    density_total = lax.psum(partial_value, "ka")
+    density_total = partial_value
+    for hop in (1, 2, 4, 8):
+        density_total = density_total + lax.ppermute(
+            density_total, "ka", [(dev, dev ^ hop) for dev in range(16)]
+        )
     screened = coulomb[:, None] * density_total
     offset = (neighbors // local_k - position + 1) % cycle_size
     local_index = offset * local_k + neighbors % local_k

time: 1170 us -> 1260 us (1.077)
  waiting for transfers between devices: 200 us -> 289 us
    ppermute x0 -> x4, waiting for transfers between devices: none -> 268 us  [on_device(): lax.ppermute(density_total, 'ka', [(dev, dev ^ hop) for dev in range(16)])]
    psum x1 -> x0, waiting for transfers between devices: 165 us -> none  [on_device(): density_total = lax.psum(partial_value, 'ka')]
    reduce_scatter x1, waiting for transfers between devices: 34.5 us -> 21.3 us  [on_device(): mine = lax.psum_scatter(pair_terms, 'ga', scatter_dimension=1, tiled=True)]
  transfers between devices with their start and end apart: 4 -> 7, of which waited for: 2 -> 5; matrix products, arithmetic and copies ran while one was open for 0% -> 0% of each run, Pallas kernels for 0% -> 0%
where the time goes in v1:
time: 1260 us
  local copies, waits for them, and re-layouts  405 us (32%)
  other arithmetic  300 us (24%)
  waiting for transfers between devices  289 us (23%)
  matrix products  242 us (19%)
  between operations  13.5 us (1%)
    add x16, other arithmetic, add_slot(): return summed + jnp.where(is_live, coupled, 0.0)  279 us
    ppermute x4, waiting for transfers between devices, on_device(): lax.ppermute(density_total, 'ka', [(dev, dev ^ hop) for dev in range(16)])  268 us
    dot_general x16, matrix products, add_slot(): jnp.einsum('kbgc,kbct->kbgt', blocks.reshape(local_k, groups, block_size,...  222 us
    gather x16, local copies, waits for them, and re-layouts, add_slot(): picked = jnp.take(window, local_index[:, slot_index], axis=0)  208 us
    gather x16, local copies, waits for them, and re-layouts, add_slot(): blocks = jnp.take(screen, q_index[:, slot_index], axis=0)  197 us
  transfers between devices with their start and end apart: 7, of which 5 were waited for; matrix products, arithmetic and copies ran while one was open for 0% of the time, Pallas kernels for 0%

profile of v1, /device:TPU:0, one launch (start us, length us, event | category | flops | bytes accessed | tf_op | source)
XLA Modules:
  0.0 1259.0 jit_solution(3145250335063060888)
XLA Ops:
  32.7 191.3 %collective-permute-done.1 = f32[2048,128]{1,0:T(8,128)S(1)} collective-permute-done((f32[2048,128]{1,0:T(8,128)S(1)}, f32[2048,128]{1,0:T(8,128)S(1)}, u32[]{:S(2)}, u32[]{:S(2)}) %collective-permute-start.1) | collective-permute-done | bytes 1048608 | tf_op jit(solution)/shard_map/ppermute | solution.py:33
  224.8 21.7 %collective-permute-done.2 = f32[2048,128]{1,0:T(8,128)S(1)} collective-permute-done((f32[2048,128]{1,0:T(8,128)S(1)}, f32[2048,128]{1,0:T(8,128)S(1)}, u32[]{:S(2)}, u32[]{:S(2)}) %collective-permute-start.2) | collective-permute-done | bytes 1048608 | tf_op jit(solution)/shard_map/ppermute | solution.py:33
  249.4 42.9 %collective-permute-done.3 = f32[2048,128]{1,0:T(8,128)S(1)} collective-permute-done((f32[2048,128]{1,0:T(8,128)S(1)}, f32[2048,128]{1,0:T(8,128)S(1)}, u32[]{:S(2)}, u32[]{:S(2)}) %collective-permute-start.3) | collective-permute-done | bytes 1048608 | tf_op jit(solution)/shard_map/ppermute | solution.py:33
  293.7 17.6 %pad_maximum_fusion = bf16[48,2048,128]{2,1,0:T(8,128)(2,1)} fusion(bf16[16,2048,128]{2,1,0:T(8,128)(2,1)} %collective-permute-done.5, bf16[16,2048,128]{2,1,0:T(8,128)(2,1)} %get-tuple-element.182, bf16[16,2048,128]{2,1,0:T(8,128)(2,1)} %collective-permute-done.4), kind=kLoop, calls=%fused_computation.19 | loop fusion | flops 25165824 | bytes 50331648 | tf_op jit(solution)/shard_map/concatenate | solution.py:29
  311.3 906.7 %while.14 = (s32[]{:T(128)}, f32[16,2048,128]{2,1,0:T(8,128)}, s32[16]{0:T(128)S(1)}, s32[16,16]{0,1:T(8,128)S(1)}, bf16[32,2048,256]{2,1,0:T(8,128)(2,1)}, /*in...) while((s32[]{:T(128)}, f32[16,2048,128]{2,1,0:T(8,128)}, ...), condition=%wide.region_2.3_spmd.clone, body=%wide.region_1.2_spmd.clone.sunk | while | flops 2172651776 | bytes 142615312 | solution.py:53
  401.6 17.8 %fusion.28 = f32[16,2048,128]{2,1,0:T(8,128)} fusion(f32[16,8,256,128]{3,2,1,0:T(8,128)} %fusion.27, f32[16,2048,128]{2,1,0:T(8,128)} %get-tuple-element.244, pred[16]{0:T(512)(128)(4,1)S(1)} %broadcast_compare_fusion.2, pred[]{:T(512)S(6)} %compare.7), kind=kLoop, calls=%fused_computation.3.clone.1 | loop fusion | flops 12582912 | bytes 50331664 | tf_op jit(solution)/shard_map/while/body/eval_jaxpr/add | solution.py:50
  458.2 17.8 %fusion.28 = f32[16,2048,128]{2,1,0:T(8,128)} fusion(f32[16,8,256,128]{3,2,1,0:T(8,128)} %fusion.27, f32[16,2048,128]{2,1,0:T(8,128)} %get-tuple-element.244, pred[16]{0:T(512)(128)(4,1)S(1)} %broadcast_compare_fusion.2, pred[]{:T(512)S(6)} %compare.7), kind=kLoop, calls=%fused_computation.3.clone.1 | loop fusion | flops 12582912 | bytes 50331664 | tf_op jit(solution)/shard_map/while/body/eval_jaxpr/add | solution.py:50
  515.0 17.8 %fusion.28 = f32[16,2048,128]{2,1,0:T(8,128)} fusion(f32[16,8,256,128]{3,2,1,0:T(8,128)} %fusion.27, f32[16,2048,128]{2,1,0:T(8,128)} %get-tuple-element.244, pred[16]{0:T(512)(128)(4,1)S(1)} %broadcast_compare_fusion.2, pred[]{:T(512)S(6)} %compare.7), kind=kLoop, calls=%fused_computation.3.clone.1 | loop fusion | flops 12582912 | bytes 50331664 | tf_op jit(solution)/shard_map/while/body/eval_jaxpr/add | solution.py:50
  571.5 17.8 %fusion.28 = f32[16,2048,128]{2,1,0:T(8,128)} fusion(f32[16,8,256,128]{3,2,1,0:T(8,128)} %fusion.27, f32[16,2048,128]{2,1,0:T(8,128)} %get-tuple-element.244, pred[16]{0:T(512)(128)(4,1)S(1)} %broadcast_compare_fusion.2, pred[]{:T(512)S(6)} %compare.7), kind=kLoop, calls=%fused_computation.3.clone.1 | loop fusion | flops 12582912 | bytes 50331664 | tf_op jit(solution)/shard_map/while/body/eval_jaxpr/add | solution.py:50
  614.2 13.9 %fusion.27 = f32[16,8,256,128]{3,2,1,0:T(8,128)} fusion(bf16[16,8,256,256]{3,2,1,0:T(8,128)(2,1)} %bitcast.29, pred[16]{0:T(512)(128)(4,1)S(1)} %get-tuple-element.231, bf16[16,8,256,128]{3,2,1,0:T(8,128)(2,1)} %bitcast.30, pred[16]{0:T(512)(128)(4,1)S(1)} %get-tuple-element.233), kind=kOutput, calls=%fused_computation.4.clone.1 | convolution fusion | flops 2160066560 | bytes 41943072 | tf_op jit(solution)/shard_map/while/body/eval_jaxpr/kbgc,kbct->kbgt/dot_general | solution.py:43
  628.1 17.8 %fusion.28 = f32[16,2048,128]{2,1,0:T(8,128)} fusion(f32[16,8,256,128]{3,2,1,0:T(8,128)} %fusion.27, f32[16,2048,128]{2,1,0:T(8,128)} %get-tuple-element.244, pred[16]{0:T(512)(128)(4,1)S(1)} %broadcast_compare_fusion.2, pred[]{:T(512)S(6)} %compare.7), kind=kLoop, calls=%fused_computation.3.clone.1 | loop fusion | flops 12582912 | bytes 50331664 | tf_op jit(solution)/shard_map/while/body/eval_jaxpr/add | solution.py:50
  684.6 17.8 %fusion.28 = f32[16,2048,128]{2,1,0:T(8,128)} fusion(f32[16,8,256,128]{3,2,1,0:T(8,128)} %fusion.27, f32[16,2048,128]{2,1,0:T(8,128)} %get-tuple-element.244, pred[16]{0:T(512)(128)(4,1)S(1)} %broadcast_compare_fusion.2, pred[]{:T(512)S(6)} %compare.7), kind=kLoop, calls=%fused_computation.3.clone.1 | loop fusion | flops 12582912 | bytes 50331664 | tf_op jit(solution)/shard_map/while/body/eval_jaxpr/add | solution.py:50
  741.7 17.8 %fusion.28 = f32[16,2048,128]{2,1,0:T(8,128)} fusion(f32[16,8,256,128]{3,2,1,0:T(8,128)} %fusion.27, f32[16,2048,128]{2,1,0:T(8,128)} %get-tuple-element.244, pred[16]{0:T(512)(128)(4,1)S(1)} %broadcast_compare_fusion.2, pred[]{:T(512)S(6)} %compare.7), kind=kLoop, calls=%fused_computation.3.clone.1 | loop fusion | flops 12582912 | bytes 50331664 | tf_op jit(solution)/shard_map/while/body/eval_jaxpr/add | solution.py:50
  798.3 17.8 %fusion.28 = f32[16,2048,128]{2,1,0:T(8,128)} fusion(f32[16,8,256,128]{3,2,1,0:T(8,128)} %fusion.27, f32[16,2048,128]{2,1,0:T(8,128)} %get-tuple-element.244, pred[16]{0:T(512)(128)(4,1)S(1)} %broadcast_compare_fusion.2, pred[]{:T(512)S(6)} %compare.7), kind=kLoop, calls=%fused_computation.3.clone.1 | loop fusion | flops 12582912 | bytes 50331664 | tf_op jit(solution)/shard_map/while/body/eval_jaxpr/add | solution.py:50
  854.8 17.8 %fusion.28 = f32[16,2048,128]{2,1,0:T(8,128)} fusion(f32[16,8,256,128]{3,2,1,0:T(8,128)} %fusion.27, f32[16,2048,128]{2,1,0:T(8,128)} %get-tuple-element.244, pred[16]{0:T(512)(128)(4,1)S(1)} %broadcast_compare_fusion.2, pred[]{:T(512)S(6)} %compare.7), kind=kLoop, calls=%fused_computation.3.clone.1 | loop fusion | flops 12582912 | bytes 50331664 | tf_op jit(solution)/shard_map/while/body/eval_jaxpr/add | solution.py:50
  897.5 13.9 %fusion.27 = f32[16,8,256,128]{3,2,1,0:T(8,128)} fusion(bf16[16,8,256,256]{3,2,1,0:T(8,128)(2,1)} %bitcast.29, pred[16]{0:T(512)(128)(4,1)S(1)} %get-tuple-element.231, bf16[16,8,256,128]{3,2,1,0:T(8,128)(2,1)} %bitcast.30, pred[16]{0:T(512)(128)(4,1)S(1)} %get-tuple-element.233), kind=kOutput, calls=%fused_computation.4.clone.1 | convolution fusion | flops 2160066560 | bytes 41943072 | tf_op jit(solution)/shard_map/while/body/eval_jaxpr/kbgc,kbct->kbgt/dot_general | solution.py:43
  911.4 17.8 %fusion.28 = f32[16,2048,128]{2,1,0:T(8,128)} fusion(f32[16,8,256,128]{3,2,1,0:T(8,128)} %fusion.27, f32[16,2048,128]{2,1,0:T(8,128)} %get-tuple-element.244, pred[16]{0:T(512)(128)(4,1)S(1)} %broadcast_compare_fusion.2, pred[]{:T(512)S(6)} %compare.7), kind=kLoop, calls=%fused_computation.3.clone.1 | loop fusion | flops 12582912 | bytes 50331664 | tf_op jit(solution)/shard_map/while/body/eval_jaxpr/add | solution.py:50
  969.8 17.8 %fusion.28 = f32[16,2048,128]{2,1,0:T(8,128)} fusion(f32[16,8,256,128]{3,2,1,0:T(8,128)} %fusion.27, f32[16,2048,128]{2,1,0:T(8,128)} %get-tuple-element.244, pred[16]{0:T(512)(128)(4,1)S(1)} %broadcast_compare_fusion.2, pred[]{:T(512)S(6)} %compare.7), kind=kLoop, calls=%fused_computation.3.clone.1 | loop fusion | flops 12582912 | bytes 50331664 | tf_op jit(solution)/shard_map/while/body/eval_jaxpr/add | solution.py:50
  1028.1 17.8 %fusion.28 = f32[16,2048,128]{2,1,0:T(8,128)} fusion(f32[16,8,256,128]{3,2,1,0:T(8,128)} %fusion.27, f32[16,2048,128]{2,1,0:T(8,128)} %get-tuple-element.244, pred[16]{0:T(512)(128)(4,1)S(1)} %broadcast_compare_fusion.2, pred[]{:T(512)S(6)} %compare.7), kind=kLoop, calls=%fused_computation.3.clone.1 | loop fusion | flops 12582912 | bytes 50331664 | tf_op jit(solution)/shard_map/while/body/eval_jaxpr/add | solution.py:50
  1085.0 17.8 %fusion.28 = f32[16,2048,128]{2,1,0:T(8,128)} fusion(f32[16,8,256,128]{3,2,1,0:T(8,128)} %fusion.27, f32[16,2048,128]{2,1,0:T(8,128)} %get-tuple-element.244, pred[16]{0:T(512)(128)(4,1)S(1)} %broadcast_compare_fusion.2, pred[]{:T(512)S(6)} %compare.7), kind=kLoop, calls=%fused_computation.3.clone.1 | loop fusion | flops 12582912 | bytes 50331664 | tf_op jit(solution)/shard_map/while/body/eval_jaxpr/add | solution.py:50
  1128.8 13.9 %fusion.27 = f32[16,8,256,128]{3,2,1,0:T(8,128)} fusion(bf16[16,8,256,256]{3,2,1,0:T(8,128)(2,1)} %bitcast.29, pred[16]{0:T(512)(128)(4,1)S(1)} %get-tuple-element.231, bf16[16,8,256,128]{3,2,1,0:T(8,128)(2,1)} %bitcast.30, pred[16]{0:T(512)(128)(4,1)S(1)} %get-tuple-element.233), kind=kOutput, calls=%fused_computation.4.clone.1 | convolution fusion | flops 2160066560 | bytes 41943072 | tf_op jit(solution)/shard_map/while/body/eval_jaxpr/kbgc,kbct->kbgt/dot_general | solution.py:43
  1142.7 17.8 %fusion.28 = f32[16,2048,128]{2,1,0:T(8,128)} fusion(f32[16,8,256,128]{3,2,1,0:T(8,128)} %fusion.27, f32[16,2048,128]{2,1,0:T(8,128)} %get-tuple-element.244, pred[16]{0:T(512)(128)(4,1)S(1)} %broadcast_compare_fusion.2, pred[]{:T(512)S(6)} %compare.7), kind=kLoop, calls=%fused_computation.3.clone.1 | loop fusion | flops 12582912 | bytes 50331664 | tf_op jit(solution)/shard_map/while/body/eval_jaxpr/add | solution.py:50
  1200.2 17.8 %fusion.28 = f32[16,2048,128]{2,1,0:T(8,128)} fusion(f32[16,8,256,128]{3,2,1,0:T(8,128)} %fusion.27, f32[16,2048,128]{2,1,0:T(8,128)} %get-tuple-element.244, pred[16]{0:T(512)(128)(4,1)S(1)} %broadcast_compare_fusion.2, pred[]{:T(512)S(6)} %compare.7), kind=kLoop, calls=%fused_computation.3.clone.1 | loop fusion | flops 12582912 | bytes 50331664 | tf_op jit(solution)/shard_map/while/body/eval_jaxpr/add | solution.py:50
  1229.2 21.3 %reduce-scatter.2.cloned.1.call-done = f32[16,32,128]{2,1,0:T(8,128)} async-done(((f32[16,64,128]{2,1,0:T(8,128)}), f32[16,32,128]{2,1,0:T(8,128)}) %reduce-scatter.2.cloned.1.call-update) | async-done | bytes 262160 | tf_op jit(solution)/shard_map/reduce_scatter | solution.py:60
  (147 shorter events, 641.5 us)
Async XLA Ops:
  6.5 1222.5 %copy-start = (f32[16,64]{1,0:T(8,128)S(1)}, f32[16,64]{1,0:T(8,128)}, u32[]{:S(2)}) copy-start(f32[16,64]{1,0:T(8,128)} %param.12) | copy-start | bytes 12292
  6.5 242.7 %copy-start.4 = (s32[16,16]{1,0:T(8,128)S(1)}, s32[16,16]{1,0:T(8,128)}, u32[]{:S(2)}) copy-start(s32[16,16]{1,0:T(8,128)} %param.15) | copy-start | bytes 3076
  6.5 242.8 %copy-start.5 = (s32[16,16]{1,0:T(8,128)S(1)}, s32[16,16]{1,0:T(8,128)}, u32[]{:S(2)}) copy-start(s32[16,16]{1,0:T(8,128)} %param.17) | copy-start | bytes 3076
  6.5 285.8 %copy-start.3 = (f32[2048]{0:T(1024)S(1)}, f32[2048]{0:T(1024)}, u32[]{:S(2)}) copy-start(f32[2048]{0:T(1024)} %param.13) | copy-start | bytes 24580
  6.5 1243.9 %reduce-scatter.2.cloned.1.call-start = ((), (), s32[]{:S(2)}) async-start(), calls=%async_computation.1 | async-start | bytes 786432 | tf_op jit(solution)/shard_map/reduce_scatter | solution.py:60
  15.2 278.4 %collective-permute-start.4 = (bf16[16,2048,128]{2,1,0:T(8,128)(2,1)}, bf16[16,2048,128]{2,1,0:T(8,128)(2,1)}, u32[]{:S(2)}, u32[]{:S(2)}) collective-permute-start(bf16[16,2048,128]{2,1,0:T(8,128)(2,1)} %get-tuple-element.182), channel_id=1, source_target_pairs={{0,2},{2,4},{4,6},{6,8},{8,10},{10,12},{12,14},{14,16},{16,18},{18... | collective-permute-start | bytes 25165832 | tf_op jit(solution)/shard_map/ppermute | solution.py:10
  15.7 278.0 %collective-permute-start.5 = (bf16[16,2048,128]{2,1,0:T(8,128)(2,1)}, bf16[16,2048,128]{2,1,0:T(8,128)(2,1)}, u32[]{:S(2)}, u32[]{:S(2)}) collective-permute-start(bf16[16,2048,128]{2,1,0:T(8,128)(2,1)} %get-tuple-element.182), channel_id=1, source_target_pairs={{0,30},{2,0},{4,2},{6,4},{8,6},{10,8},{12,10},{14,12},{16,14},{18,... | collective-permute-start | bytes 25165832 | tf_op jit(solution)/shard_map/ppermute | solution.py:10
  20.7 11.8 collective-permute-start
  32.6 191.4 %collective-permute-start.1 = (f32[2048,128]{1,0:T(8,128)S(1)}, f32[2048,128]{1,0:T(8,128)S(1)}, u32[]{:S(2)}, u32[]{:S(2)}) collective-permute-start(f32[2048,128]{1,0:T(8,128)S(1)} %add.93), channel_id=1, source_target_pairs={{0,4},{2,6},{4,0},{6,2},{8,12},{10,14},{12,8},{14,10},{16,20},{18,... | collective-permute-start | bytes 3145736 | tf_op jit(solution)/shard_map/ppermute | solution.py:33
  224.0 22.5 %collective-permute-start.2 = (f32[2048,128]{1,0:T(8,128)S(1)}, f32[2048,128]{1,0:T(8,128)S(1)}, u32[]{:S(2)}, u32[]{:S(2)}) collective-permute-start(f32[2048,128]{1,0:T(8,128)S(1)} %add.94), channel_id=1, source_target_pairs={{0,8},{2,10},{4,12},{6,14},{8,0},{10,2},{12,4},{14,6},{16,24},{18,... | collective-permute-start | bytes 3145736 | tf_op jit(solution)/shard_map/ppermute | solution.py:33
  246.6 45.8 %collective-permute-start.3 = (f32[2048,128]{1,0:T(8,128)S(1)}, f32[2048,128]{1,0:T(8,128)S(1)}, u32[]{:S(2)}, u32[]{:S(2)}) collective-permute-start(f32[2048,128]{1,0:T(8,128)S(1)} %add.95), channel_id=1, source_target_pairs={{0,16},{2,18},{4,20},{6,22},{8,24},{10,26},{12,28},{14,30},{16,0},... | collective-permute-start | bytes 3145736 | tf_op jit(solution)/shard_map/ppermute | solution.py:33
  293.7 17.6 %copy-start.6 = (s32[16]{0:T(128)S(1)}, s32[16]{0:T(128)}, u32[]{:S(2)}) copy-start(s32[16]{0:T(128)} %param.16) | copy-start | bytes 196
  311.2 906.7 %copy-start.1 = (f32[2048,128]{1,0:T(8,128)S(1)}, f32[2048,128]{1,0:T(8,128)}, u32[]{:S(2)}) copy-start(f32[2048,128]{1,0:T(8,128)} %multiply_multiply_fusion) | copy-start | bytes 3145732
  1218.0 32.5 %copy-start.2 = (bf16[16,64,128]{2,1,0:T(8,128)(2,1)S(1)}, bf16[16,64,128]{2,1,0:T(8,128)(2,1)}, u32[]{:S(2)}) copy-start(bf16[16,64,128]{2,1,0:T(8,128)(2,1)} %param.11) | copy-start | bytes 786436
Sparse Core Ops, SparseCore 0:
  1229.2 21.2 reduce-scatter.1
